TPU v7x, 32 devices: a whole 2x2x4 slice. The times are simulated.
32 devices in a mesh: slab: 4 (over x, core), panel: 8 (over z, y).
Axes of the slice: x: 2, y: 2, z: 4, core: 2. Of those that a mesh axis runs over, the one named last changes fastest.
Arguments:
- ranges: float32 [4, 4, 1024, 1024], P('slab', None, 'panel'), may hold values from -1.5 to 1.5
- pattern: int32 [4, 4, 16, 16], P('slab'), may hold values 0 or 1
Outputs:
- combined: float32 [4, 4, 1024, 1024], P('slab', None, 'panel')
All inputs are finite; a program needn't handle non-finite values. No bound on the sum of `pattern` on one device may be relied on, other than what follows from the above.
Results may differ from a plain program's by a relative error of at most 0.01.
Values may be sent and summed in bfloat16 or wider, within the bound.
A program may use at most 64 MiB of HBM per device.

v0:
```python
import jax
import jax.numpy as jnp
from jax import lax
from jax.sharding import PartitionSpec as P

M = 1024
BLK = 64
LEVELS = 2


def partner_2(block, axis, distance):
    count = lax.axis_size(axis)
    route = []
    for low in range(count):
        high = low | 1 << distance
        if high != low and high < count:
            route += [(low, high), (high, low)]
    return lax.ppermute(block, axis, route)


def to_half(values):
    return values.astype(jnp.bfloat16)


def star(head, tail, tree_level, row_start):
    head_top, head_up, head_down, head_bottom = (head[0], head[1], head[2], head[3])
    tail_top, tail_up, tail_down, tail_bottom = (tail[0], tail[1], tail[2], tail[3])
    local_rows = head.shape[1]
    col_side = lax.axis_index("slab") >> tree_level & 1
    col_start = col_side * (M // 2)

    def cut_cols(values):
        return lax.dynamic_slice_in_dim(to_half(values), col_start, M // 2, 1)

    right_bottom, right_up, right_down = (
        lax.all_gather(cut_cols(head_bottom), "panel", axis=0, tiled=True),
        lax.all_gather(cut_cols(tail_up), "panel", axis=0, tiled=True),
        lax.all_gather(cut_cols(head_down), "panel", axis=0, tiled=True),
    )

    def spread(values):
        return lax.all_gather(cut_cols(values), "panel", axis=0, tiled=True)

    def multiply(left, right):
        half_cols = jnp.dot(to_half(left), right, preferred_element_type=jnp.float32)
        other_cols = partner_2(half_cols, "slab", tree_level)
        return jnp.where(
            col_side == 0,
            jnp.concatenate([half_cols, other_cols], 1),
            jnp.concatenate([other_cols, half_cols], 1),
        )

    col_ids = col_start + jnp.arange(M // 2, dtype=jnp.int32)
    all_ids = jnp.arange(M, dtype=jnp.int32)
    eye_right = (all_ids[:, None] == col_ids[None, :]).astype(jnp.float32)
    row_ids = row_start + jnp.arange(local_rows, dtype=jnp.int32)
    eye_rows = (row_ids[:, None] == all_ids[None, :]).astype(jnp.float32)
    loop_term = multiply(tail_top, right_bottom)
    loop_kept = lax.optimization_barrier(to_half(loop_term)).astype(jnp.float32)
    right_loop = spread(loop_term)
    right_defect = to_half(eye_right - right_loop.astype(jnp.float32))
    right_guess = to_half(eye_right + right_loop.astype(jnp.float32))
    guess = eye_rows + loop_kept
    guess = 2.0 * guess - multiply(multiply(guess, right_defect), right_guess)
    right_inverse = spread(guess)
    lifted = multiply(head_up, right_inverse)
    joint_up = multiply(lifted, right_up)
    bounce = multiply(tail_top, right_down)
    right_bounce = spread(bounce)
    joint_top = head_top + multiply(lifted, right_bounce)
    reach = multiply(tail_down, right_bottom)
    through = multiply(reach, right_inverse)
    joint_down = multiply(tail_down, right_down) + multiply(through, right_bounce)
    joint_bottom = (
        tail_bottom + multiply(reach, right_up) + multiply(multiply(through, right_loop), right_up)
    )
    return jnp.stack([joint_top, joint_up, joint_down, joint_bottom])


def body(ranges, pattern):
    group_blocks = ranges[0]
    local_rows = group_blocks.shape[1]
    block_count = pattern.shape[2]
    row_start = lax.axis_index("panel") * local_rows
    row_ids = row_start + jnp.arange(local_rows, dtype=jnp.int32)
    col_ids = jnp.arange(M, dtype=jnp.int32)
    block_ids = jnp.arange(block_count, dtype=jnp.int32)
    row_pick = (row_ids[:, None] // BLK == block_ids[None, :]).astype(jnp.float32)
    col_pick = (block_ids[:, None] == col_ids[None, :] // BLK).astype(jnp.float32)
    block_mask = jnp.einsum("mi,gij,jc->gmc", row_pick, pattern[0].astype(jnp.float32), col_pick)
    merged = group_blocks * block_mask
    for tree_level in range(LEVELS):
        partner = partner_2(merged, "slab", tree_level)
        is_lower = lax.axis_index("slab") >> tree_level & 1 == 0
        head_blocks = jnp.where(is_lower, merged, partner)
        tail_blocks = jnp.where(is_lower, partner, merged)
        merged = star(head_blocks, tail_blocks, tree_level, row_start)
    return merged[None]


def solution(mesh):
    return jax.shard_map(
        body,
        mesh=mesh,
        in_specs=(P("slab", None, "panel", None), P("slab", None, None, None)),
        out_specs=P("slab", None, "panel", None),
        check_vma=False,
    )
```

profile of v0, /device:TPU:0, one launch (start us, length us, event | category | flops | bytes accessed | tf_op | source)
XLA Modules:
  0.0 616.8 jit_solution(5166546670370426008)
XLA Ops:
  6.6 2.3 bitcast_multiply_fusion
  9.4 3.9 collective-permute-done
  13.3 4.4 fusion.131
  19.5 43.0 %all-gather.31.cloned.1.call-done = bf16[1,1024,512]{2,1,0:T(8,128)(2,1)} async-done(((bf16[1,128,512]{2,1,0:T(8,128)(2,1)}), bf16[1,1024,512]{2,1,0:T(8,128)(2,1)}) %all-gather.31.cloned.1.call-update) | async-done | bytes 1048592 | tf_op jit(solution)/shard_map/all_gather | solution.py:36
  67.8 37.5 %all-gather.19.cloned.1.call-done = bf16[1024,512]{1,0:T(8,128)(2,1)} async-done(((bf16[128,512]{1,0:T(8,128)(2,1)}), bf16[1024,512]{1,0:T(8,128)(2,1)}) %all-gather.19.cloned.1.call-update) | async-done | bytes 1048592 | tf_op jit(solution)/shard_map/all_gather | solution.py:42
  105.4 1.9 fusion.10
  111.7 34.8 %all-gather.33.cloned.1.call-done = bf16[1,1024,512]{2,1,0:T(8,128)(2,1)} async-done(((bf16[1,128,512]{2,1,0:T(8,128)(2,1)}), bf16[1,1024,512]{2,1,0:T(8,128)(2,1)}) %all-gather.33.cloned.1.call-update) | async-done | bytes 1048592 | tf_op jit(solution)/shard_map/all_gather | solution.py:38
  146.5 1.6 fusion.34
  151.7 35.8 %all-gather.35.cloned.1.call-done = bf16[1,1024,512]{2,1,0:T(8,128)(2,1)} async-done(((bf16[1,128,512]{2,1,0:T(8,128)(2,1)}), bf16[1,1024,512]{2,1,0:T(8,128)(2,1)}) %all-gather.35.cloned.1.call-update) | async-done | bytes 1048592 | tf_op jit(solution)/shard_map/all_gather | solution.py:37
  189.2 39.4 %all-gather.21.cloned.1.call-done = bf16[1024,512]{1,0:T(8,128)(2,1)} async-done(((bf16[128,512]{1,0:T(8,128)(2,1)}), bf16[1024,512]{1,0:T(8,128)(2,1)}) %all-gather.21.cloned.1.call-update) | async-done | bytes 1048592 | tf_op jit(solution)/shard_map/all_gather | solution.py:42
  228.6 1.7 fusion.124
  232.6 37.0 %all-gather.23.cloned.1.call-done = bf16[1024,512]{1,0:T(8,128)(2,1)} async-done(((bf16[128,512]{1,0:T(8,128)(2,1)}), bf16[1024,512]{1,0:T(8,128)(2,1)}) %all-gather.23.cloned.1.call-update) | async-done | bytes 1048592 | tf_op jit(solution)/shard_map/all_gather | solution.py:42
  269.6 1.6 fusion.127
  279.7 46.5 %collective-permute-done.15 = f32[4,128,1024]{2,1,0:T(8,128)} collective-permute-done((f32[4,128,1024]{2,1,0:T(8,128)}, f32[4,128,1024]{2,1,0:T(8,128)}, u32[]{:S(2)}, u32[]{:S(2)}) %collective-permute-start.15) | collective-permute-done | bytes 2097184 | tf_op jit(solution)/shard_map/ppermute | solution.py:18
  326.2 4.4 fusion.129
  332.4 39.1 %all-gather.37.cloned.1.call-done = bf16[1,1024,512]{2,1,0:T(8,128)(2,1)} async-done(((bf16[1,128,512]{2,1,0:T(8,128)(2,1)}), bf16[1,1024,512]{2,1,0:T(8,128)(2,1)}) %all-gather.37.cloned.1.call-update) | async-done | bytes 1048592 | tf_op jit(solution)/shard_map/all_gather | solution.py:36
  374.6 3.5 collective-permute-done.16
  380.5 37.6 %all-gather.25.cloned.1.call-done = bf16[1024,512]{1,0:T(8,128)(2,1)} async-done(((bf16[128,512]{1,0:T(8,128)(2,1)}), bf16[1024,512]{1,0:T(8,128)(2,1)}) %all-gather.25.cloned.1.call-update) | async-done | bytes 1048592 | tf_op jit(solution)/shard_map/all_gather | solution.py:42
  418.0 1.9 fusion.6
  421.4 3.5 collective-permute-done.17
  427.2 4.7 collective-permute-done.18
  433.0 26.2 %all-gather.39.cloned.1.call-done = bf16[1,1024,512]{2,1,0:T(8,128)(2,1)} async-done(((bf16[1,128,512]{2,1,0:T(8,128)(2,1)}), bf16[1,1024,512]{2,1,0:T(8,128)(2,1)}) %all-gather.39.cloned.1.call-update) | async-done | bytes 1048592 | tf_op jit(solution)/shard_map/all_gather | solution.py:38
  459.2 1.6 fusion.20
  462.3 3.5 collective-permute-done.20
  469.4 30.8 %all-gather.41.cloned.1.call-done = bf16[1,1024,512]{2,1,0:T(8,128)(2,1)} async-done(((bf16[1,128,512]{2,1,0:T(8,128)(2,1)}), bf16[1,1024,512]{2,1,0:T(8,128)(2,1)}) %all-gather.41.cloned.1.call-update) | async-done | bytes 1048592 | tf_op jit(solution)/shard_map/all_gather | solution.py:37
  503.2 38.1 %all-gather.27.cloned.1.call-done = bf16[1024,512]{1,0:T(8,128)(2,1)} async-done(((bf16[128,512]{1,0:T(8,128)(2,1)}), bf16[1024,512]{1,0:T(8,128)(2,1)}) %all-gather.27.cloned.1.call-update) | async-done | bytes 1048592 | tf_op jit(solution)/shard_map/all_gather | solution.py:42
  541.3 1.7 fusion.114
  546.5 3.0 collective-permute-done.25
  550.3 32.0 %all-gather.29.cloned.1.call-done = bf16[1024,512]{1,0:T(8,128)(2,1)} async-done(((bf16[128,512]{1,0:T(8,128)(2,1)}), bf16[1024,512]{1,0:T(8,128)(2,1)}) %all-gather.29.cloned.1.call-update) | async-done | bytes 1048592 | tf_op jit(solution)/shard_map/all_gather | solution.py:42
  582.3 1.6 fusion.117
  588.6 10.2 %collective-permute-done.22 = f32[128,512]{1,0:T(8,128)S(1)} collective-permute-done((f32[128,512]{1,0:T(8,128)S(1)}, f32[128,512]{1,0:T(8,128)S(1)}, u32[]{:S(2)}, u32[]{:S(2)}) %collective-permute-start.22) | collective-permute-done | bytes 262176 | tf_op jit(solution)/shard_map/ppermute | solution.py:18
  600.3 4.1 collective-permute-done.26
  (164 shorter events, 63.7 us)
Async XLA Ops:
  6.5 56.0 %all-gather.31.cloned.1.call-start = ((), (), s32[]{:S(2)}) async-start(), calls=%async_computation.6 | async-start | bytes 1179648 | tf_op jit(solution)/shard_map/all_gather | solution.py:36
  19.5 85.9 %all-gather.19.cloned.1.call-start = ((), (), s32[]{:S(2)}) async-start(), calls=%async_computation | async-start | bytes 1179648 | tf_op jit(solution)/shard_map/all_gather | solution.py:42
  66.2 80.3 %all-gather.33.cloned.1.call-start = ((), (), s32[]{:S(2)}) async-start(), calls=%async_computation.7 | async-start | bytes 1179648 | tf_op jit(solution)/shard_map/all_gather | solution.py:38
  67.0 120.6 %all-gather.35.cloned.1.call-start = ((), (), s32[]{:S(2)}) async-start(), calls=%async_computation.8 | async-start | bytes 1179648 | tf_op jit(solution)/shard_map/all_gather | solution.py:37
  67.8 160.8 %all-gather.21.cloned.1.call-start = ((), (), s32[]{:S(2)}) async-start(), calls=%async_computation.1 | async-start | bytes 1179648 | tf_op jit(solution)/shard_map/all_gather | solution.py:42
  111.7 157.9 %all-gather.23.cloned.1.call-start = ((), (), s32[]{:S(2)}) async-start(), calls=%async_computation.2 | async-start | bytes 1179648 | tf_op jit(solution)/shard_map/all_gather | solution.py:42
  150.4 221.2 %all-gather.37.cloned.1.call-start = ((), (), s32[]{:S(2)}) async-start(), calls=%async_computation.9 | async-start | bytes 1179648 | tf_op jit(solution)/shard_map/all_gather | solution.py:36
  150.7 36.8 %collective-permute-start.9 = (bf16[128,512]{1,0:T(8,128)(2,1)S(1)}, bf16[128,512]{1,0:T(8,128)(2,1)S(1)}, u32[]{:S(2)}, u32[]{:S(2)}) collective-permute-start(bf16[128,512]{1,0:T(8,128)(2,1)S(1)} %fusion.36), channel_id=1, source_target_pairs={{0,8},{8,0},{16,24},{24,16},{1,9},{9,1},{17,25},{25,17},{2,10},{10... | collective-permute-start | bytes 393224 | tf_op jit(solution)/shard_map/ppermute | solution.py:18
  151.3 122.5 %collective-permute-start.8 = (f32[128,512]{1,0:T(8,128)S(1)}, f32[128,512]{1,0:T(8,128)S(1)}, u32[]{:S(2)}, u32[]{:S(2)}) collective-permute-start(f32[128,512]{1,0:T(8,128)S(1)} %fusion.32), channel_id=1, source_target_pairs={{0,8},{8,0},{16,24},{24,16},{1,9},{9,1},{17,25},{25,17},{2,10},{10... | collective-permute-start | bytes 786440 | tf_op jit(solution)/shard_map/ppermute | solution.py:18
  189.1 86.4 %collective-permute-start.12 = (f32[128,512]{1,0:T(8,128)S(1)}, f32[128,512]{1,0:T(8,128)S(1)}, u32[]{:S(2)}, u32[]{:S(2)}) collective-permute-start(f32[128,512]{1,0:T(8,128)S(1)} %fusion.28), channel_id=1, source_target_pairs={{0,8},{8,0},{16,24},{24,16},{1,9},{9,1},{17,25},{25,17},{2,10},{10... | collective-permute-start | bytes 786440 | tf_op jit(solution)/shard_map/ppermute | solution.py:18
  231.6 38.0 %collective-permute-start.4 = (bf16[128,512]{1,0:T(8,128)(2,1)S(1)}, bf16[128,512]{1,0:T(8,128)(2,1)S(1)}, u32[]{:S(2)}, u32[]{:S(2)}) collective-permute-start(bf16[128,512]{1,0:T(8,128)(2,1)S(1)} %fusion.83), channel_id=1, source_target_pairs={{0,8},{8,0},{16,24},{24,16},{1,9},{9,1},{17,25},{25,17},{2,10},{10... | collective-permute-start | bytes 393224 | tf_op jit(solution)/shard_map/ppermute | solution.py:18
  232.5 40.0 %collective-permute-start.13 = (bf16[128,512]{1,0:T(8,128)(2,1)S(1)}, bf16[128,512]{1,0:T(8,128)(2,1)S(1)}, u32[]{:S(2)}, u32[]{:S(2)}) collective-permute-start(bf16[128,512]{1,0:T(8,128)(2,1)S(1)} %fusion.119), channel_id=1, source_target_pairs={{0,8},{8,0},{16,24},{24,16},{1,9},{9,1},{17,25},{25,17},{2,10},{10... | collective-permute-start | bytes 393224 | tf_op jit(solution)/shard_map/ppermute | solution.py:18
  278.3 48.0 %collective-permute-start.15 = (f32[4,128,1024]{2,1,0:T(8,128)}, f32[4,128,1024]{2,1,0:T(8,128)}, u32[]{:S(2)}, u32[]{:S(2)}) collective-permute-start(f32[4,128,1024]{2,1,0:T(8,128)} %pad_maximum_fusion), channel_id=1, source_target_pairs={{0,16},{16,0},{8,24},{24,8},{1,17},{17,1},{9,25},{25,9},{2,18},{18... | collective-permute-start | bytes 6291464 | tf_op jit(solution)/shard_map/ppermute | solution.py:18
  332.4 85.6 %all-gather.25.cloned.1.call-start = ((), (), s32[]{:S(2)}) async-start(), calls=%async_computation.3 | async-start | bytes 1179648 | tf_op jit(solution)/shard_map/all_gather | solution.py:42
  373.1 5.0 collective-permute-start.16
  378.9 80.3 %all-gather.39.cloned.1.call-start = ((), (), s32[]{:S(2)}) async-start(), calls=%async_computation.10 | async-start | bytes 1179648 | tf_op jit(solution)/shard_map/all_gather | solution.py:38
  379.6 120.5 %all-gather.41.cloned.1.call-start = ((), (), s32[]{:S(2)}) async-start(), calls=%async_computation.11 | async-start | bytes 1179648 | tf_op jit(solution)/shard_map/all_gather | solution.py:37
  380.4 160.9 %all-gather.27.cloned.1.call-start = ((), (), s32[]{:S(2)}) async-start(), calls=%async_computation.4 | async-start | bytes 1179648 | tf_op jit(solution)/shard_map/all_gather | solution.py:42
  419.9 5.0 collective-permute-start.17
  425.5 6.4 %collective-permute-start.18 = (f32[128,512]{1,0:T(8,128)S(1)}, f32[128,512]{1,0:T(8,128)S(1)}, u32[]{:S(2)}, u32[]{:S(2)}) collective-permute-start(f32[128,512]{1,0:T(8,128)S(1)} %fusion.4), channel_id=1, source_target_pairs={{0,16},{16,0},{8,24},{24,8},{1,17},{17,1},{9,25},{25,9},{2,18},{18... | collective-permute-start | bytes 786440 | tf_op jit(solution)/shard_map/ppermute | solution.py:18
  432.7 149.6 %all-gather.29.cloned.1.call-start = ((), (), s32[]{:S(2)}) async-start(), calls=%async_computation.5 | async-start | bytes 1179648 | tf_op jit(solution)/shard_map/all_gather | solution.py:42
  460.8 5.0 collective-permute-start.20
  466.9 33.2 %collective-permute-start.24 = (bf16[128,512]{1,0:T(8,128)(2,1)S(1)}, bf16[128,512]{1,0:T(8,128)(2,1)S(1)}, u32[]{:S(2)}, u32[]{:S(2)}) collective-permute-start(bf16[128,512]{1,0:T(8,128)(2,1)S(1)} %fusion.22), channel_id=1, source_target_pairs={{0,16},{16,0},{8,24},{24,8},{1,17},{17,1},{9,25},{25,9},{2,18},{18... | collective-permute-start | bytes 393224 | tf_op jit(solution)/shard_map/ppermute | solution.py:18
  468.8 131.6 %collective-permute-start.23 = (f32[128,512]{1,0:T(8,128)S(1)}, f32[128,512]{1,0:T(8,128)S(1)}, u32[]{:S(2)}, u32[]{:S(2)}) collective-permute-start(f32[128,512]{1,0:T(8,128)S(1)} %fusion.18), channel_id=1, source_target_pairs={{0,16},{16,0},{8,24},{24,8},{1,17},{17,1},{9,25},{25,9},{2,18},{18... | collective-permute-start | bytes 786440 | tf_op jit(solution)/shard_map/ppermute | solution.py:18
  501.7 104.1 %collective-permute-start.27 = (f32[128,512]{1,0:T(8,128)S(1)}, f32[128,512]{1,0:T(8,128)S(1)}, u32[]{:S(2)}, u32[]{:S(2)}) collective-permute-start(f32[128,512]{1,0:T(8,128)S(1)} %fusion.14), channel_id=1, source_target_pairs={{0,16},{16,0},{8,24},{24,8},{1,17},{17,1},{9,25},{25,9},{2,18},{18... | collective-permute-start | bytes 786440 | tf_op jit(solution)/shard_map/ppermute | solution.py:18
  543.0 6.4 %collective-permute-start.25 = (bf16[128,512]{1,0:T(8,128)(2,1)S(1)}, bf16[128,512]{1,0:T(8,128)(2,1)S(1)}, u32[]{:S(2)}, u32[]{:S(2)}) collective-permute-start(bf16[128,512]{1,0:T(8,128)(2,1)S(1)} %fusion.114), channel_id=1, source_target_pairs={{0,16},{16,0},{8,24},{24,8},{1,17},{17,1},{9,25},{25,9},{2,18},{18... | collective-permute-start | bytes 393224 | tf_op jit(solution)/shard_map/ppermute | solution.py:18
  545.8 36.5 %collective-permute-start.19 = (bf16[128,512]{1,0:T(8,128)(2,1)S(1)}, bf16[128,512]{1,0:T(8,128)(2,1)S(1)}, u32[]{:S(2)}, u32[]{:S(2)}) collective-permute-start(bf16[128,512]{1,0:T(8,128)(2,1)S(1)} %fusion.82), channel_id=1, source_target_pairs={{0,16},{16,0},{8,24},{24,8},{1,17},{17,1},{9,25},{25,9},{2,18},{18... | collective-permute-start | bytes 393224 | tf_op jit(solution)/shard_map/ppermute | solution.py:18
  549.8 37.0 %collective-permute-start.28 = (bf16[128,512]{1,0:T(8,128)(2,1)S(1)}, bf16[128,512]{1,0:T(8,128)(2,1)S(1)}, u32[]{:S(2)}, u32[]{:S(2)}) collective-permute-start(bf16[128,512]{1,0:T(8,128)(2,1)S(1)} %fusion.109), channel_id=1, source_target_pairs={{0,16},{16,0},{8,24},{24,8},{1,17},{17,1},{9,25},{25,9},{2,18},{18... | collective-permute-start | bytes 393224 | tf_op jit(solution)/shard_map/ppermute | solution.py:18
  583.9 20.7 %collective-permute-start.21 = (f32[128,512]{1,0:T(8,128)S(1)}, f32[128,512]{1,0:T(8,128)S(1)}, u32[]{:S(2)}, u32[]{:S(2)}) collective-permute-start(f32[128,512]{1,0:T(8,128)S(1)} %fusion.117), channel_id=1, source_target_pairs={{0,16},{16,0},{8,24},{24,8},{1,17},{17,1},{9,25},{25,9},{2,18},{18... | collective-permute-start | bytes 786440 | tf_op jit(solution)/shard_map/ppermute | solution.py:18
  585.8 13.0 %collective-permute-start.22 = (f32[128,512]{1,0:T(8,128)S(1)}, f32[128,512]{1,0:T(8,128)S(1)}, u32[]{:S(2)}, u32[]{:S(2)}) collective-permute-start(f32[128,512]{1,0:T(8,128)S(1)} %fusion.16), channel_id=1, source_target_pairs={{0,16},{16,0},{8,24},{24,8},{1,17},{17,1},{9,25},{25,9},{2,18},{18... | collective-permute-start | bytes 786440 | tf_op jit(solution)/shard_map/ppermute | solution.py:18
  586.8 17.7 %collective-permute-start.26 = (f32[128,512]{1,0:T(8,128)S(1)}, f32[128,512]{1,0:T(8,128)S(1)}, u32[]{:S(2)}, u32[]{:S(2)}) collective-permute-start(f32[128,512]{1,0:T(8,128)S(1)} %fusion.111), channel_id=1, source_target_pairs={{0,16},{16,0},{8,24},{24,8},{1,17},{17,1},{9,25},{25,9},{2,18},{18... | collective-permute-start | bytes 786440 | tf_op jit(solution)/shard_map/ppermute | solution.py:18
  598.8 8.4 %collective-permute-start.29 = (f32[128,512]{1,0:T(8,128)S(1)}, f32[128,512]{1,0:T(8,128)S(1)}, u32[]{:S(2)}, u32[]{:S(2)}) collective-permute-start(f32[128,512]{1,0:T(8,128)S(1)} %fusion.12), channel_id=1, source_target_pairs={{0,16},{16,0},{8,24},{24,8},{1,17},{17,1},{9,25},{25,9},{2,18},{18... | collective-permute-start | bytes 786440 | tf_op jit(solution)/shard_map/ppermute | solution.py:18
  (27 other events, 233.3 us)
Sparse Core Ops, SparseCore 0:
  19.6 42.8 all-gather.30
  66.4 38.9 all-gather.18
  107.5 38.9 all-gather.32
  148.5 38.9 all-gather.34
  189.5 38.9 all-gather.20
  230.5 39.0 all-gather.22
  332.5 38.9 all-gather.36
  379.0 38.9 all-gather.24
  420.2 38.9 all-gather.38
  461.1 38.9 all-gather.40
  502.3 38.9 all-gather.26
  543.3 38.9 all-gather.28
where the time goes:
time: 618 us; the launch traced here: 617 us
  waiting for transfers between devices  522 us (84%)
  matrix products  29.3 us (5%)
  starting transfers between devices  23.3 us (4%)
  other arithmetic  20.7 us (3%)
  between operations  14.1 us (2%)
  local copies, waits for them, and re-layouts  7.5 us (1%)
    all_gather x6, waiting for transfers between devices, spread(): return lax.all_gather(cut_cols(values), 'panel', axis=0, tiled=True)  222 us
    ppermute x30, waiting for transfers between devices, partner_2(): return lax.ppermute(block, axis, route)  90.4 us
    all_gather x2, waiting for transfers between devices, star(): lax.all_gather(cut_cols(head_bottom), 'panel', axis=0, tiled=True)  82.1 us
    all_gather x2, waiting for transfers between devices, star(): lax.all_gather(cut_cols(tail_up), 'panel', axis=0, tiled=True)  66.6 us
    all_gather x2, waiting for transfers between devices, star(): lax.all_gather(cut_cols(head_down), 'panel', axis=0, tiled=True)  61 us
    dot_general x28, matrix products, multiply(): jnp.dot(to_half(left), right, preferred_element_type=jnp.float32)  27 us
    ppermute x30, starting transfers between devices, partner_2(): return lax.ppermute(block, axis, route)  22.7 us
  transfers between devices with their start and end apart: 42, of which 28 were waited for; matrix products, arithmetic and copies ran while one was open for 5% of the time, Pallas kernels for 0%

commit v1 on v0

--- a/solution.py
+++ b/solution.py
@@ -6,6 +6,24 @@
 M = 1024
 BLK = 64
 LEVELS = 2
+
+
+def collect(shard, axis, dim):
+    ways, here, hop = (lax.axis_size(axis), lax.axis_index(axis), shard.shape[dim])
+    dims = [n * ways if d == dim else n for d, n in enumerate(shard.shape)]
+    full = lax.dynamic_update_slice_in_dim(
+        jnp.zeros(dims, shard.dtype), shard, here * hop, axis=dim
+    )
+    going_up = going_down = shard
+    for far in range(1, ways // 2 + 1):
+        going_up = lax.ppermute(going_up, axis, [(d, (d + 1) % ways) for d in range(ways)])
+        full = lax.dynamic_update_slice_in_dim(full, going_up, (here - far) % ways * hop, axis=dim)
+        if 2 * far < ways:
+            going_down = lax.ppermute(going_down, axis, [(d, (d - 1) % ways) for d in range(ways)])
+            full = lax.dynamic_update_slice_in_dim(
+                full, going_down, (here + far) % ways * hop, axis=dim
+            )
+    return full
 
 
 def partner_2(block, axis, distance):
@@ -33,7 +51,7 @@
         return lax.dynamic_slice_in_dim(to_half(values), col_start, M // 2, 1)
 
     right_bottom, right_up, right_down = (
-        lax.all_gather(cut_cols(head_bottom), "panel", axis=0, tiled=True),
+        collect(cut_cols(head_bottom), "panel", 0),
         lax.all_gather(cut_cols(tail_up), "panel", axis=0, tiled=True),
         lax.all_gather(cut_cols(head_down), "panel", axis=0, tiled=True),
     )

time: 618 us -> 595 us (0.963)
  waiting for transfers between devices: 522 us -> 473 us
  starting transfers between devices: 23.3 us -> 53.5 us
    all_gather x2 -> x0, waiting for transfers between devices: 82.1 us -> none  [star(): lax.all_gather(cut_cols(head_bottom), 'panel', axis=0, tiled=True)]
    ppermute x0 -> x14, waiting for transfers between devices: none -> 35.1 us  [the longest x8 34.8 us: collect(): lax.ppermute(going_up, axis, [(d, (d + 1) % ways) for d in range(ways)])]
    ppermute x0 -> x14, starting transfers between devices: none -> 30.2 us  [the longest x6 23.4 us: collect(): lax.ppermute(going_down, axis, [(d, (d - 1) % ways) for d in range(ways)])]
  transfers between devices with their start and end apart: 42 -> 54, of which waited for: 28 -> 37; matrix products, arithmetic and copies ran while one was open for 5% -> 6% of each run, Pallas kernels for 0% -> 0%
where the time goes in v1:
time: 595 us
  waiting for transfers between devices  473 us (79%)
  starting transfers between devices  53.5 us (9%)
  matrix products  27.4 us (5%)
  other arithmetic  21 us (4%)
  between operations  14.2 us (2%)
    all_gather x6, waiting for transfers between devices, spread(): return lax.all_gather(cut_cols(values), 'panel', axis=0, tiled=True)  218 us
    ppermute x30, waiting for transfers between devices, partner_2(): return lax.ppermute(block, axis, route)  94.9 us
    all_gather x2, waiting for transfers between devices, star(): lax.all_gather(cut_cols(tail_up), 'panel', axis=0, tiled=True)  64.1 us
    all_gather x2, waiting for transfers between devices, star(): lax.all_gather(cut_cols(head_down), 'panel', axis=0, tiled=True)  61.1 us
    ppermute x8, waiting for transfers between devices, collect(): lax.ppermute(going_up, axis, [(d, (d + 1) % ways) for d in range(ways)])  34.8 us
    dot_general x28, matrix products, multiply(): jnp.dot(to_half(left), right, preferred_element_type=jnp.float32)  25.1 us
    ppermute x6, starting transfers between devices, collect(): lax.ppermute(going_down, axis, [(d, (d - 1) % ways) for d in range(ways)])  23.4 us
    ppermute x30, starting transfers between devices, partner_2(): return lax.ppermute(block, axis, route)  22.8 us
  transfers between devices with their start and end apart: 54, of which 37 were waited for; matrix products, arithmetic and copies ran while one was open for 6% of the time, Pallas kernels for 0%

profile of v1, /device:TPU:0, one launch (start us, length us, event | category | flops | bytes accessed | tf_op | source)
XLA Modules:
  0.0 594.5 jit_solution(7306875062331463406)
XLA Ops:
  9.4 3.9 collective-permute-done
  13.3 4.4 fusion.127
  21.6 3.0 collective-permute-start.2
  24.6 3.9 collective-permute-done.1
  29.9 3.3 collective-permute-start.4
  37.8 4.0 collective-permute-start.6
  44.7 8.8 %collective-permute-done.7 = bf16[128,512]{1,0:T(8,128)(2,1)S(1)} collective-permute-done((bf16[128,512]{1,0:T(8,128)(2,1)S(1)}, bf16[128,512]{1,0:T(8,128)(2,1)S(1)}, u32[]{:S(2)}, u32[]{:S(2)}) %collective-permute-start.7) | collective-permute-done | bytes 131104 | tf_op jit(solution)/shard_map/ppermute | solution.py:19
  57.6 37.6 %all-gather.15.cloned.1.call-done = bf16[1024,512]{1,0:T(8,128)(2,1)} async-done(((bf16[128,512]{1,0:T(8,128)(2,1)}), bf16[1024,512]{1,0:T(8,128)(2,1)}) %all-gather.15.cloned.1.call-update) | async-done | bytes 1048592 | tf_op jit(solution)/shard_map/all_gather | solution.py:60
  101.5 34.9 %all-gather.27.cloned.1.call-done = bf16[1,1024,512]{2,1,0:T(8,128)(2,1)} async-done(((bf16[1,128,512]{2,1,0:T(8,128)(2,1)}), bf16[1,1024,512]{2,1,0:T(8,128)(2,1)}) %all-gather.27.cloned.1.call-update) | async-done | bytes 1048592 | tf_op jit(solution)/shard_map/all_gather | solution.py:56
  141.9 35.7 %all-gather.29.cloned.1.call-done = bf16[1,1024,512]{2,1,0:T(8,128)(2,1)} async-done(((bf16[1,128,512]{2,1,0:T(8,128)(2,1)}), bf16[1,1024,512]{2,1,0:T(8,128)(2,1)}) %all-gather.29.cloned.1.call-update) | async-done | bytes 1048592 | tf_op jit(solution)/shard_map/all_gather | solution.py:55
  180.7 37.9 %all-gather.17.cloned.1.call-done = bf16[1024,512]{1,0:T(8,128)(2,1)} async-done(((bf16[128,512]{1,0:T(8,128)(2,1)}), bf16[1024,512]{1,0:T(8,128)(2,1)}) %all-gather.17.cloned.1.call-update) | async-done | bytes 1048592 | tf_op jit(solution)/shard_map/all_gather | solution.py:60
  222.6 37.0 %all-gather.19.cloned.1.call-done = bf16[1024,512]{1,0:T(8,128)(2,1)} async-done(((bf16[128,512]{1,0:T(8,128)(2,1)}), bf16[1024,512]{1,0:T(8,128)(2,1)}) %all-gather.19.cloned.1.call-update) | async-done | bytes 1048592 | tf_op jit(solution)/shard_map/all_gather | solution.py:60
  269.9 46.5 %collective-permute-done.22 = f32[4,128,1024]{2,1,0:T(8,128)} collective-permute-done((f32[4,128,1024]{2,1,0:T(8,128)}, f32[4,128,1024]{2,1,0:T(8,128)}, u32[]{:S(2)}, u32[]{:S(2)}) %collective-permute-start.22) | collective-permute-done | bytes 2097184 | tf_op jit(solution)/shard_map/ppermute | solution.py:36
  316.4 4.4 fusion.125
  321.6 4.1 collective-permute-start.24
  325.7 2.9 collective-permute-done.23
  329.4 4.1 collective-permute-start.26
  336.5 4.8 collective-permute-start.28
  344.2 7.6 %collective-permute-done.29 = bf16[128,512]{1,0:T(8,128)(2,1)S(1)} collective-permute-done((bf16[128,512]{1,0:T(8,128)(2,1)S(1)}, bf16[128,512]{1,0:T(8,128)(2,1)S(1)}, u32[]{:S(2)}, u32[]{:S(2)}) %collective-permute-start.29) | collective-permute-done | bytes 131104 | tf_op jit(solution)/shard_map/ppermute | solution.py:19
  353.6 3.5 collective-permute-done.30
  359.5 36.1 %all-gather.21.cloned.1.call-done = bf16[1024,512]{1,0:T(8,128)(2,1)} async-done(((bf16[128,512]{1,0:T(8,128)(2,1)}), bf16[1024,512]{1,0:T(8,128)(2,1)}) %all-gather.21.cloned.1.call-update) | async-done | bytes 1048592 | tf_op jit(solution)/shard_map/all_gather | solution.py:60
  399.0 3.5 collective-permute-done.31
  404.7 4.7 collective-permute-done.32
  410.5 26.2 %all-gather.31.cloned.1.call-done = bf16[1,1024,512]{2,1,0:T(8,128)(2,1)} async-done(((bf16[1,128,512]{2,1,0:T(8,128)(2,1)}), bf16[1,1024,512]{2,1,0:T(8,128)(2,1)}) %all-gather.31.cloned.1.call-update) | async-done | bytes 1048592 | tf_op jit(solution)/shard_map/all_gather | solution.py:56
  439.8 3.5 collective-permute-done.34
  445.9 3.5 collective-permute-done.38
  449.4 28.4 %all-gather.33.cloned.1.call-done = bf16[1,1024,512]{2,1,0:T(8,128)(2,1)} async-done(((bf16[1,128,512]{2,1,0:T(8,128)(2,1)}), bf16[1,1024,512]{2,1,0:T(8,128)(2,1)}) %all-gather.33.cloned.1.call-update) | async-done | bytes 1048592 | tf_op jit(solution)/shard_map/all_gather | solution.py:55
  481.9 37.1 %all-gather.23.cloned.1.call-done = bf16[1024,512]{1,0:T(8,128)(2,1)} async-done(((bf16[128,512]{1,0:T(8,128)(2,1)}), bf16[1024,512]{1,0:T(8,128)(2,1)}) %all-gather.23.cloned.1.call-update) | async-done | bytes 1048592 | tf_op jit(solution)/shard_map/all_gather | solution.py:60
  524.2 3.0 collective-permute-done.39
  528.0 32.0 %all-gather.25.cloned.1.call-done = bf16[1024,512]{1,0:T(8,128)(2,1)} async-done(((bf16[128,512]{1,0:T(8,128)(2,1)}), bf16[1024,512]{1,0:T(8,128)(2,1)}) %all-gather.25.cloned.1.call-update) | async-done | bytes 1048592 | tf_op jit(solution)/shard_map/all_gather | solution.py:60
  566.3 10.2 %collective-permute-done.36 = f32[128,512]{1,0:T(8,128)S(1)} collective-permute-done((f32[128,512]{1,0:T(8,128)S(1)}, f32[128,512]{1,0:T(8,128)S(1)}, u32[]{:S(2)}, u32[]{:S(2)}) %collective-permute-start.36) | collective-permute-done | bytes 262176 | tf_op jit(solution)/shard_map/ppermute | solution.py:36
  578.2 3.9 collective-permute-done.35
  (198 shorter events, 95.8 us)
Async XLA Ops:
  6.5 88.7 %all-gather.15.cloned.1.call-start = ((), (), s32[]{:S(2)}) async-start(), calls=%async_computation | async-start | bytes 1179648 | tf_op jit(solution)/shard_map/all_gather | solution.py:60
  18.7 9.8 %collective-permute-start.1 = (bf16[128,512]{1,0:T(8,128)(2,1)S(1)}, bf16[128,512]{1,0:T(8,128)(2,1)S(1)}, u32[]{:S(2)}, u32[]{:S(2)}) collective-permute-start(bf16[128,512]{1,0:T(8,128)(2,1)S(1)} %get-tuple-element.12), channel_id=1, source_target_pairs={{0,1},{1,2},{2,3},{3,4},{4,5},{5,6},{6,7},{7,0},{8,9},{9,10},{10,1... | collective-permute-start | bytes 393224 | tf_op jit(solution)/shard_map/ppermute | solution.py:19
  21.6 8.4 %collective-permute-start.2 = (bf16[128,512]{1,0:T(8,128)(2,1)S(1)}, bf16[128,512]{1,0:T(8,128)(2,1)S(1)}, u32[]{:S(2)}, u32[]{:S(2)}) collective-permute-start(bf16[128,512]{1,0:T(8,128)(2,1)S(1)} %get-tuple-element.12), channel_id=1, source_target_pairs={{0,7},{1,0},{2,1},{3,2},{4,3},{5,4},{6,5},{7,6},{8,15},{9,8},{10,9... | collective-permute-start | bytes 393224 | tf_op jit(solution)/shard_map/ppermute | solution.py:22
  28.5 7.7 %collective-permute-start.3 = (bf16[128,512]{1,0:T(8,128)(2,1)S(1)}, bf16[128,512]{1,0:T(8,128)(2,1)S(1)}, u32[]{:S(2)}, u32[]{:S(2)}) collective-permute-start(bf16[128,512]{1,0:T(8,128)(2,1)S(1)} %collective-permute-done.1), channel_id=1, source_target_pairs={{0,1},{1,2},{2,3},{3,4},{4,5},{5,6},{6,7},{7,0},{8,9},{9,10},{10,1... | collective-permute-start | bytes 393224 | tf_op jit(solution)/shard_map/ppermute | solution.py:19
  29.9 7.8 %collective-permute-start.4 = (bf16[128,512]{1,0:T(8,128)(2,1)S(1)}, bf16[128,512]{1,0:T(8,128)(2,1)S(1)}, u32[]{:S(2)}, u32[]{:S(2)}) collective-permute-start(bf16[128,512]{1,0:T(8,128)(2,1)S(1)} %collective-permute-done.2), channel_id=1, source_target_pairs={{0,7},{1,0},{2,1},{3,2},{4,3},{5,4},{6,5},{7,6},{8,15},{9,8},{10,9... | collective-permute-start | bytes 393224 | tf_op jit(solution)/shard_map/ppermute | solution.py:22
  36.2 8.5 %collective-permute-start.5 = (bf16[128,512]{1,0:T(8,128)(2,1)S(1)}, bf16[128,512]{1,0:T(8,128)(2,1)S(1)}, u32[]{:S(2)}, u32[]{:S(2)}) collective-permute-start(bf16[128,512]{1,0:T(8,128)(2,1)S(1)} %collective-permute-done.3), channel_id=1, source_target_pairs={{0,1},{1,2},{2,3},{3,4},{4,5},{5,6},{6,7},{7,0},{8,9},{9,10},{10,1... | collective-permute-start | bytes 393224 | tf_op jit(solution)/shard_map/ppermute | solution.py:19
  44.7 8.8 %collective-permute-start.7 = (bf16[128,512]{1,0:T(8,128)(2,1)S(1)}, bf16[128,512]{1,0:T(8,128)(2,1)S(1)}, u32[]{:S(2)}, u32[]{:S(2)}) collective-permute-start(bf16[128,512]{1,0:T(8,128)(2,1)S(1)} %collective-permute-done.5), channel_id=1, source_target_pairs={{0,1},{1,2},{2,3},{3,4},{4,5},{5,6},{6,7},{7,0},{8,9},{9,10},{10,1... | collective-permute-start | bytes 393224 | tf_op jit(solution)/shard_map/ppermute | solution.py:19
  56.0 80.3 %all-gather.27.cloned.1.call-start = ((), (), s32[]{:S(2)}) async-start(), calls=%async_computation.6 | async-start | bytes 1179648 | tf_op jit(solution)/shard_map/all_gather | solution.py:56
  56.8 120.8 %all-gather.29.cloned.1.call-start = ((), (), s32[]{:S(2)}) async-start(), calls=%async_computation.7 | async-start | bytes 1179648 | tf_op jit(solution)/shard_map/all_gather | solution.py:55
  57.6 161.0 %all-gather.17.cloned.1.call-start = ((), (), s32[]{:S(2)}) async-start(), calls=%async_computation.1 | async-start | bytes 1179648 | tf_op jit(solution)/shard_map/all_gather | solution.py:60
  101.4 158.2 %all-gather.19.cloned.1.call-start = ((), (), s32[]{:S(2)}) async-start(), calls=%async_computation.2 | async-start | bytes 1179648 | tf_op jit(solution)/shard_map/all_gather | solution.py:60
  140.1 255.5 %all-gather.21.cloned.1.call-start = ((), (), s32[]{:S(2)}) async-start(), calls=%async_computation.3 | async-start | bytes 1179648 | tf_op jit(solution)/shard_map/all_gather | solution.py:60
  179.8 85.5 %collective-permute-start.19 = (f32[128,512]{1,0:T(8,128)}, f32[128,512]{1,0:T(8,128)}, u32[]{:S(2)}, u32[]{:S(2)}) collective-permute-start(f32[128,512]{1,0:T(8,128)} %fusion.24), channel_id=1, source_target_pairs={{0,8},{8,0},{16,24},{24,16},{1,9},{9,1},{17,25},{25,17},{2,10},{10... | collective-permute-start | bytes 786440 | tf_op jit(solution)/shard_map/ppermute | solution.py:36
  180.1 83.7 %collective-permute-start.15 = (f32[128,512]{1,0:T(8,128)S(1)}, f32[128,512]{1,0:T(8,128)S(1)}, u32[]{:S(2)}, u32[]{:S(2)}) collective-permute-start(f32[128,512]{1,0:T(8,128)S(1)} %fusion.28), channel_id=1, source_target_pairs={{0,8},{8,0},{16,24},{24,16},{1,9},{9,1},{17,25},{25,17},{2,10},{10... | collective-permute-start | bytes 786440 | tf_op jit(solution)/shard_map/ppermute | solution.py:36
  221.6 39.7 %collective-permute-start.11 = (bf16[128,512]{1,0:T(8,128)(2,1)S(1)}, bf16[128,512]{1,0:T(8,128)(2,1)S(1)}, u32[]{:S(2)}, u32[]{:S(2)}) collective-permute-start(bf16[128,512]{1,0:T(8,128)(2,1)S(1)} %fusion.75), channel_id=1, source_target_pairs={{0,8},{8,0},{16,24},{24,16},{1,9},{9,1},{17,25},{25,17},{2,10},{10... | collective-permute-start | bytes 393224 | tf_op jit(solution)/shard_map/ppermute | solution.py:36
  222.5 40.0 %collective-permute-start.20 = (bf16[128,512]{1,0:T(8,128)(2,1)S(1)}, bf16[128,512]{1,0:T(8,128)(2,1)S(1)}, u32[]{:S(2)}, u32[]{:S(2)}) collective-permute-start(bf16[128,512]{1,0:T(8,128)(2,1)S(1)} %fusion.115), channel_id=1, source_target_pairs={{0,8},{8,0},{16,24},{24,16},{1,9},{9,1},{17,25},{25,17},{2,10},{10... | collective-permute-start | bytes 393224 | tf_op jit(solution)/shard_map/ppermute | solution.py:36
  268.4 48.0 %collective-permute-start.22 = (f32[4,128,1024]{2,1,0:T(8,128)}, f32[4,128,1024]{2,1,0:T(8,128)}, u32[]{:S(2)}, u32[]{:S(2)}) collective-permute-start(f32[4,128,1024]{2,1,0:T(8,128)} %pad_maximum_fusion), channel_id=1, source_target_pairs={{0,16},{16,0},{8,24},{24,8},{1,17},{17,1},{9,25},{25,9},{2,18},{18... | collective-permute-start | bytes 6291464 | tf_op jit(solution)/shard_map/ppermute | solution.py:36
  321.0 7.7 %collective-permute-start.23 = (bf16[128,512]{1,0:T(8,128)(2,1)S(1)}, bf16[128,512]{1,0:T(8,128)(2,1)S(1)}, u32[]{:S(2)}, u32[]{:S(2)}) collective-permute-start(bf16[128,512]{1,0:T(8,128)(2,1)S(1)} %get-tuple-element.6), channel_id=1, source_target_pairs={{0,1},{1,2},{2,3},{3,4},{4,5},{5,6},{6,7},{7,0},{8,9},{9,10},{10,1... | collective-permute-start | bytes 393224 | tf_op jit(solution)/shard_map/ppermute | solution.py:19
  321.6 7.8 %collective-permute-start.24 = (bf16[128,512]{1,0:T(8,128)(2,1)S(1)}, bf16[128,512]{1,0:T(8,128)(2,1)S(1)}, u32[]{:S(2)}, u32[]{:S(2)}) collective-permute-start(bf16[128,512]{1,0:T(8,128)(2,1)S(1)} %get-tuple-element.6), channel_id=1, source_target_pairs={{0,7},{1,0},{2,1},{3,2},{4,3},{5,4},{6,5},{7,6},{8,15},{9,8},{10,9... | collective-permute-start | bytes 393224 | tf_op jit(solution)/shard_map/ppermute | solution.py:22
  328.7 7.8 %collective-permute-start.25 = (bf16[128,512]{1,0:T(8,128)(2,1)S(1)}, bf16[128,512]{1,0:T(8,128)(2,1)S(1)}, u32[]{:S(2)}, u32[]{:S(2)}) collective-permute-start(bf16[128,512]{1,0:T(8,128)(2,1)S(1)} %collective-permute-done.23), channel_id=1, source_target_pairs={{0,1},{1,2},{2,3},{3,4},{4,5},{5,6},{6,7},{7,0},{8,9},{9,10},{10,1... | collective-permute-start | bytes 393224 | tf_op jit(solution)/shard_map/ppermute | solution.py:19
  357.9 78.8 %all-gather.31.cloned.1.call-start = ((), (), s32[]{:S(2)}) async-start(), calls=%async_computation.8 | async-start | bytes 1179648 | tf_op jit(solution)/shard_map/all_gather | solution.py:56
  358.7 119.2 %all-gather.33.cloned.1.call-start = ((), (), s32[]{:S(2)}) async-start(), calls=%async_computation.9 | async-start | bytes 1179648 | tf_op jit(solution)/shard_map/all_gather | solution.py:55
  359.4 159.6 %all-gather.23.cloned.1.call-start = ((), (), s32[]{:S(2)}) async-start(), calls=%async_computation.4 | async-start | bytes 1179648 | tf_op jit(solution)/shard_map/all_gather | solution.py:60
  410.3 149.7 %all-gather.25.cloned.1.call-start = ((), (), s32[]{:S(2)}) async-start(), calls=%async_computation.5 | async-start | bytes 1179648 | tf_op jit(solution)/shard_map/all_gather | solution.py:60
  479.4 103.9 %collective-permute-start.41 = (f32[128,512]{1,0:T(8,128)S(1)}, f32[128,512]{1,0:T(8,128)S(1)}, u32[]{:S(2)}, u32[]{:S(2)}) collective-permute-start(f32[128,512]{1,0:T(8,128)S(1)} %fusion.14), channel_id=1, source_target_pairs={{0,16},{16,0},{8,24},{24,8},{1,17},{17,1},{9,25},{25,9},{2,18},{18... | collective-permute-start | bytes 786440 | tf_op jit(solution)/shard_map/ppermute | solution.py:36
  481.3 96.8 %collective-permute-start.37 = (f32[128,512]{1,0:T(8,128)S(1)}, f32[128,512]{1,0:T(8,128)S(1)}, u32[]{:S(2)}, u32[]{:S(2)}) collective-permute-start(f32[128,512]{1,0:T(8,128)S(1)} %fusion.18), channel_id=1, source_target_pairs={{0,16},{16,0},{8,24},{24,8},{1,17},{17,1},{9,25},{25,9},{2,18},{18... | collective-permute-start | bytes 786440 | tf_op jit(solution)/shard_map/ppermute | solution.py:36
  523.5 39.6 %collective-permute-start.33 = (bf16[128,512]{1,0:T(8,128)(2,1)S(1)}, bf16[128,512]{1,0:T(8,128)(2,1)S(1)}, u32[]{:S(2)}, u32[]{:S(2)}) collective-permute-start(bf16[128,512]{1,0:T(8,128)(2,1)S(1)} %fusion.74), channel_id=1, source_target_pairs={{0,16},{16,0},{8,24},{24,8},{1,17},{17,1},{9,25},{25,9},{2,18},{18... | collective-permute-start | bytes 393224 | tf_op jit(solution)/shard_map/ppermute | solution.py:36
  527.5 37.0 %collective-permute-start.42 = (bf16[128,512]{1,0:T(8,128)(2,1)S(1)}, bf16[128,512]{1,0:T(8,128)(2,1)S(1)}, u32[]{:S(2)}, u32[]{:S(2)}) collective-permute-start(bf16[128,512]{1,0:T(8,128)(2,1)S(1)} %fusion.105), channel_id=1, source_target_pairs={{0,16},{16,0},{8,24},{24,8},{1,17},{17,1},{9,25},{25,9},{2,18},{18... | collective-permute-start | bytes 393224 | tf_op jit(solution)/shard_map/ppermute | solution.py:36
  561.7 16.4 %collective-permute-start.40 = (f32[128,512]{1,0:T(8,128)S(1)}, f32[128,512]{1,0:T(8,128)S(1)}, u32[]{:S(2)}, u32[]{:S(2)}) collective-permute-start(f32[128,512]{1,0:T(8,128)S(1)} %fusion.107), channel_id=1, source_target_pairs={{0,16},{16,0},{8,24},{24,8},{1,17},{17,1},{9,25},{25,9},{2,18},{18... | collective-permute-start | bytes 786440 | tf_op jit(solution)/shard_map/ppermute | solution.py:36
  563.5 13.0 %collective-permute-start.36 = (f32[128,512]{1,0:T(8,128)S(1)}, f32[128,512]{1,0:T(8,128)S(1)}, u32[]{:S(2)}, u32[]{:S(2)}) collective-permute-start(f32[128,512]{1,0:T(8,128)S(1)} %fusion.16), channel_id=1, source_target_pairs={{0,16},{16,0},{8,24},{24,8},{1,17},{17,1},{9,25},{25,9},{2,18},{18... | collective-permute-start | bytes 786440 | tf_op jit(solution)/shard_map/ppermute | solution.py:36
  564.5 17.6 %collective-permute-start.35 = (f32[128,512]{1,0:T(8,128)S(1)}, f32[128,512]{1,0:T(8,128)S(1)}, u32[]{:S(2)}, u32[]{:S(2)}) collective-permute-start(f32[128,512]{1,0:T(8,128)S(1)} %fusion.113), channel_id=1, source_target_pairs={{0,16},{16,0},{8,24},{24,8},{1,17},{17,1},{9,25},{25,9},{2,18},{18... | collective-permute-start | bytes 786440 | tf_op jit(solution)/shard_map/ppermute | solution.py:36
  576.5 8.4 %collective-permute-start.43 = (f32[128,512]{1,0:T(8,128)S(1)}, f32[128,512]{1,0:T(8,128)S(1)}, u32[]{:S(2)}, u32[]{:S(2)}) collective-permute-start(f32[128,512]{1,0:T(8,128)S(1)} %fusion.12), channel_id=1, source_target_pairs={{0,16},{16,0},{8,24},{24,8},{1,17},{17,1},{9,25},{25,9},{2,18},{18... | collective-permute-start | bytes 786440 | tf_op jit(solution)/shard_map/ppermute | solution.py:36
  (37 other events, 322.5 us)
Sparse Core Ops, SparseCore 0:
  56.2 38.9 all-gather.14
  97.3 38.9 all-gather.26
  138.5 39.0 all-gather.28
  179.5 38.9 all-gather.16
  220.5 39.0 all-gather.18
  358.0 37.4 all-gather.20
  397.7 38.9 all-gather.30
  438.9 38.9 all-gather.32
  480.0 38.9 all-gather.22
  521.0 38.9 all-gather.24
